TPU v7x, 32 devices: a whole 2x2x4 slice. The times are simulated.
32 devices in a mesh: freq: 2 (over x), src: 16 (over z, y, core).
Axes of the slice: x: 2, y: 2, z: 4, core: 2. Of those that a mesh axis runs over, the one named last changes fastest.
Arguments:
- shots: bfloat16 [4, 8192, 8192], P('freq', 'src'), parts along dimension 0, may hold values from -6 to 6
- wavelet: float32 [4, 8192], P('freq', 'src'), parts along dimension 0, may hold values from -1.2 to 1.2
- obliquity: float32 [8192], P('src'), may hold values from 0.3 to 3
- aperture: int32 [64, 64, 4], P('src'), may hold values from -1 to 63, as said below
Outputs:
- multiples: bfloat16 [4, 8192, 8192], P('freq', None, 'src'), parts along dimension 0
There are 2 independent parts, one for each index of `freq`. A program takes and returns all parts, laid end to end along the dimension named above; an argument that names none is the same for every part. Nothing has to cross between parts.
Inputs may be any that keep to these rules, and one draw needn't show every extreme that they name: `aperture`: entry (i, j, t) is -1 (unused) or a block k with |k - j| <= 2; no block stands twice in one list.
All inputs are finite; a program needn't handle non-finite values.
Results may differ from a plain program's by a relative error of at most 0.0072.
Values may be sent and summed in bfloat16 or wider, within the bound.
A program may use at most 192 MiB of HBM per device.

v0:
```python
import jax
import jax.numpy as jnp
from jax import lax
from jax.sharding import PartitionSpec as P

BLK = 128
APW = 2


def block_column(lefts, rights, mask_col, row_count):
    row_blocks = row_count // BLK
    window_len = len(lefts)
    left_all = jnp.stack(lefts, axis=2).reshape(2, row_blocks, BLK, window_len, BLK)
    left_all = left_all * mask_col.astype(jnp.bfloat16)[None, :, None, :, None]
    left_all = left_all.reshape(2, row_count, window_len * BLK)
    left_big = jnp.concatenate([left_all[0], left_all[1]], axis=1)
    right_re = jnp.concatenate([r[0] for r in rights], axis=0)
    right_im = jnp.concatenate([r[1] for r in rights], axis=0)
    right_big = jnp.concatenate(
        [
            jnp.concatenate([right_re, right_im], axis=1),
            jnp.concatenate([-right_im, right_re], axis=1),
        ],
        axis=0,
    )
    product = jnp.dot(left_big, right_big, preferred_element_type=jnp.float32)
    return -jnp.stack([product[:, :BLK], product[:, BLK:]])


def valid_targets(targets, block_total):
    return jnp.where((targets >= 0) & (targets < block_total), targets, -2)


def per_device(shots, wavelet, obliquity, aperture):
    shot_re = shots[0].astype(jnp.float32)
    shot_im = shots[1].astype(jnp.float32)
    wave_re = wavelet[0][:, None]
    wave_im = wavelet[1][:, None]
    scaled = jnp.stack(
        [shot_re * wave_re - shot_im * wave_im, shot_re * wave_im + shot_im * wave_re]
    ).astype(jnp.bfloat16)
    window_len = 2 * APW + 1
    offsets = jnp.arange(window_len, dtype=jnp.int32) - APW
    scales = lax.all_gather(obliquity, "src", axis=0, tiled=True)
    data = (scaled.astype(jnp.float32) * scales).astype(jnp.bfloat16)
    row_count = data.shape[1]
    row_blocks = row_count // BLK
    block_count = data.shape[2] // BLK
    base_block = lax.axis_index("src") * row_blocks
    band_rows = []
    for r in range(row_blocks):
        row_pieces = []
        for u in range(window_len):
            c_block = jnp.clip(base_block + r + u - APW, 0, block_count - 1)
            row_pieces.append(
                lax.dynamic_slice(
                    data, (jnp.int32(0), jnp.int32(r * BLK), c_block * BLK), (2, BLK, BLK)
                )
            )
        band_rows.append(jnp.stack(row_pieces))
    band_local = jnp.stack(band_rows)
    band_all = lax.all_gather(band_local, "src", axis=0, tiled=True)
    column_ids = jnp.arange(block_count, dtype=jnp.int32)
    targets_all = valid_targets(column_ids[:, None] + offsets[None, :], block_count)
    mask_all = jnp.any(aperture[:, :, :, None] == targets_all[None, :, None, :], axis=2)

    def one_group(g, output):
        for u in range(8):
            j = g * 8 + u
            mask_col = lax.dynamic_index_in_dim(mask_all, j, 1, keepdims=False)
            lefts = []
            rights = []
            for w in range(window_len):
                k_block = jnp.clip(j + w - APW, 0, block_count - 1)
                lefts.append(
                    lax.dynamic_slice(
                        data, (jnp.int32(0), jnp.int32(0), k_block * BLK), (2, row_count, BLK)
                    )
                )
                rights.append(
                    lax.dynamic_index_in_dim(
                        lax.dynamic_index_in_dim(band_all, k_block, 0, keepdims=False),
                        2 * APW - w,
                        0,
                        keepdims=False,
                    )
                )
            column = block_column(lefts, rights, mask_col, row_count).astype(jnp.bfloat16)
            output = lax.dynamic_update_slice(output, column, (jnp.int32(0), jnp.int32(0), j * BLK))
        return output

    rows_result = lax.fori_loop(
        0, block_count // 8, one_group, jnp.zeros((2, row_count, block_count * BLK), jnp.bfloat16)
    )
    return lax.all_to_all(rows_result, "src", split_axis=2, concat_axis=1, tiled=True)


def solution(mesh):
    return jax.shard_map(
        per_device,
        mesh=mesh,
        in_specs=(P("freq", "src", None), P("freq", "src"), P("src"), P("src", None, None)),
        out_specs=P("freq", None, "src"),
        check_vma=False,
    )
```

profile of v0, /device:TPU:1, one launch (start us, length us, event | category | flops | bytes accessed | tf_op | source)
XLA Modules:
  0.0 1068.1 jit_solution(2346869558573901106)
XLA Ops:
  7.3 23.3 %all-gather = f32[16,1,512]{2,1,0:T(1,128)S(1)} all-gather(f32[1,1,512]{2,1,0:T(1,128)} %bitcast.648), channel_id=1, replica_groups=mesh['freq'=2,'src'=16] {'src'}, dimensions={0}, use_global_device_ids=true | all-gather | bytes 34816 | tf_op jit(solution)/shard_map/all_gather | solution.py:44
  30.6 11.8 %fusion.144 = (bf16[1,512,8192]{2,1,0:T(8,128)(2,1)}, bf16[1,512,8192]{2,1,0:T(8,128)(2,1)}) fusion(bf16[2,512,8192]{2,1,0:T(8,128)(2,1)} %param.6), kind=kLoop, calls=%fused_computation.461 | loop fusion | bytes 33554432 | tf_op jit(solution)/shard_map/slice | solution.py:36
  42.4 11.9 %copy.114 = bf16[1,512,8192]{1,2,0:T(8,128)(2,1)} copy(bf16[1,512,8192]{2,1,0:T(8,128)(2,1)} %get-tuple-element.547) | data formatting | bytes 16777216
  54.3 11.9 %copy.113 = bf16[1,512,8192]{1,2,0:T(8,128)(2,1)} copy(bf16[1,512,8192]{2,1,0:T(8,128)(2,1)} %get-tuple-element.548) | data formatting | bytes 16777216
  66.2 8.8 fusion.129
  75.0 3.3 multiply_convert_fusion
  78.3 5.8 copy-done
  87.5 1.2 pad_maximum_fusion
  89.6 105.3 %all-gather.3.cloned.1.call-done = bf16[64,5,2,128,128]{4,3,2,1,0:T(8,128)(2,1)} async-done(((bf16[4,5,2,128,128]{4,3,2,1,0:T(8,128)(2,1)}), bf16[64,5,2,128,128]{4,3,2,1,0:T(8,128)(2,1)}) %all-gather.3.cloned.1.call-update) | async-done | bytes 20971536 | tf_op jit(solution)/shard_map/all_gather | solution.py:62
  194.9 6.1 broadcast_in_dim.36
  201.0 410.3 %while.18 = (s32[]{:T(128)}, bf16[2,512,8192]{2,1,0:T(8,128)(2,1)}, bf16[2,512,8192]{1,2,0:T(8,128)(2,1)}, pred[4,64,5]{2,0,1:T(4,128)(4,1)S(1)}, bf16[64,5,2,12...) while((s32[]{:T(128)}, bf16[2,512,8192]{2,1,0:T(8,128)(2,1)}, ...), condition=%wide.region_2.3_spmd, body=%wide.region_1.2_spmd.sunk | while | flops 2735341824 | bytes 156504944 | solution.py:92
  205.3 1.2 constant_dynamic-update-slice_fusion.150
  210.2 1.1 constant_dynamic-update-slice_fusion.155
  216.9 2.1 constant_dynamic-slice_fusion.41
  256.6 1.2 constant_dynamic-update-slice_fusion.150
  261.5 1.1 constant_dynamic-update-slice_fusion.155
  268.2 2.1 constant_dynamic-slice_fusion.41
  307.9 1.2 constant_dynamic-update-slice_fusion.150
  319.5 2.1 constant_dynamic-slice_fusion.41
  359.2 1.2 constant_dynamic-update-slice_fusion.150
  370.8 2.1 constant_dynamic-slice_fusion.41
  410.4 1.2 constant_dynamic-update-slice_fusion.150
  422.0 2.1 constant_dynamic-slice_fusion.41
  461.7 1.2 constant_dynamic-update-slice_fusion.150
  473.3 2.1 constant_dynamic-slice_fusion.41
  513.0 1.2 constant_dynamic-update-slice_fusion.150
  524.6 2.1 constant_dynamic-slice_fusion.41
  564.3 1.2 constant_dynamic-update-slice_fusion.150
  575.9 2.1 constant_dynamic-slice_fusion.41
  611.3 40.9 %copy.111 = bf16[2,512,8192]{1,0,2:T(2,128)(2,1)} copy(bf16[2,512,8192]{2,1,0:T(8,128)(2,1)} %get-tuple-element.323) | data formatting | bytes 33554432 | tf_op jit(solution)/shard_map/while | solution.py:92
  652.2 368.3 %all_to_all.18 = bf16[2,512,8192]{1,0,2:T(2,128)(2,1)} all-to-all(bf16[2,512,8192]{1,0,2:T(2,128)(2,1)} %copy.111), channel_id=1, replica_groups=mesh['freq'=2,'src'=16] {'src'}, dimensions={2} | all-to-all | bytes 33554432 | tf_op jit(solution)/shard_map/all_to_all | solution.py:95
  1020.5 40.8 %copy.112 = bf16[2,16,512,512]{3,2,1,0:T(8,128)(2,1)} copy(bf16[2,16,512,512]{2,0,3,1:T(2,128)(2,1)} %bitcast.624) | data formatting | bytes 33554432 | tf_op jit(solution)/shard_map/all_to_all | solution.py:95
  (1465 shorter events, 379.9 us)
Async XLA Ops:
  6.5 188.4 %all-gather.3.cloned.1.call-start = ((), (), s32[]{:S(2)}) async-start(), calls=%async_computation.1 | async-start | bytes 22282240 | tf_op jit(solution)/shard_map/all_gather | solution.py:62
  78.3 5.8 copy-start
  206.5 4.7 copy-start.13
  206.5 4.7 copy-start.15
  206.5 4.7 copy-start.37
  206.6 4.7 copy-start.39
  210.2 5.3 copy-start.35
  257.8 4.7 copy-start.13
  257.8 4.7 copy-start.15
  257.8 4.7 copy-start.37
  257.8 4.7 copy-start.39
  261.4 5.3 copy-start.35
  309.1 4.7 copy-start.13
  309.1 4.7 copy-start.15
  312.7 5.3 copy-start.35
  360.4 4.7 copy-start.13
  360.4 4.7 copy-start.15
  360.4 4.7 copy-start.37
  360.4 4.7 copy-start.39
  364.0 5.3 copy-start.35
  415.3 5.3 copy-start.35
  466.6 5.3 copy-start.35
  514.2 4.8 copy-start.13
  514.2 4.8 copy-start.15
  514.2 4.8 copy-start.37
  514.2 4.8 copy-start.39
  517.9 5.3 copy-start.35
  565.5 4.7 copy-start.13
  565.5 4.7 copy-start.15
  565.5 4.7 copy-start.37
  565.5 4.7 copy-start.39
  569.1 5.3 copy-start.35
  (291 other events, 569.2 us)
Sparse Core Ops, SparseCore 0:
  88.9 106.0 all-gather.2
where the time goes:
time: 1080 us; the launch traced here: 1070 us
  blocking collectives  392 us (36%)
  local copies, waits for them, and re-layouts  367 us (34%)
  other arithmetic  149 us (14%)
  waiting for transfers between devices  105 us (10%)
  matrix products  34.8 us (3%)
  between operations  13.7 us (1%)
    all_to_all x1, blocking collectives, per_device(): lax.all_to_all(rows_result, 'src', split_axis=2, concat_axis=1, tiled=True)  368 us
    while x792, local copies, waits for them, and re-layouts  145 us
    all_gather x1, waiting for transfers between devices, per_device(): band_all = lax.all_gather(band_local, 'src', axis=0, tiled=True)  105 us
    dynamic_update_slice x64, other arithmetic, one_group(): lax.dynamic_update_slice(output, column, (jnp.int32(0), jnp.int32(0), j *...  48 us
    neg x64, other arithmetic, block_column(): -right_im  47.3 us
    while x2, local copies, waits for them, and re-layouts, per_device(): lax.fori_loop(0, block_count // 8, one_group, jnp.zeros((2, row_count, bl...  41 us
    all_to_all x1, local copies, waits for them, and re-layouts, per_device(): lax.all_to_all(rows_result, 'src', split_axis=2, concat_axis=1, tiled=True)  40.8 us
    mul x64, other arithmetic, block_column(): left_all = left_all * mask_col.astype(jnp.bfloat16)[None, :, None, :, None]  39.8 us
  transfers between devices with their start and end apart: 1, of which 1 were waited for; matrix products, arithmetic and copies ran while one was open for 0% of the time, Pallas kernels for 0%

commit v1 on v0

--- a/solution.py
+++ b/solution.py
@@ -5,6 +5,18 @@
 
 BLK = 128
 APW = 2
+
+
+def doubled_up(array, axis, dim):
+    ways, here = (lax.axis_size(axis), lax.axis_index(axis))
+    grown, reach = (array, 1)
+    while reach < ways:
+        theirs = lax.ppermute(grown, axis, [(d, d ^ reach) for d in range(ways)])
+        mine_first = jnp.concatenate([grown, theirs], axis=dim)
+        theirs_first = jnp.concatenate([theirs, grown], axis=dim)
+        grown = jnp.where(here & reach == 0, mine_first, theirs_first)
+        reach = 2 * reach
+    return grown
 
 
 def block_column(lefts, rights, mask_col, row_count):
@@ -59,7 +71,7 @@
             )
         band_rows.append(jnp.stack(row_pieces))
     band_local = jnp.stack(band_rows)
-    band_all = lax.all_gather(band_local, "src", axis=0, tiled=True)
+    band_all = doubled_up(band_local, "src", 0)
     column_ids = jnp.arange(block_count, dtype=jnp.int32)
     targets_all = valid_targets(column_ids[:, None] + offsets[None, :], block_count)
     mask_all = jnp.any(aperture[:, :, :, None] == targets_all[None, :, None, :], axis=2)

time: 1080 us -> 1630 us (1.51)
  waiting for transfers between devices: 105 us -> 628 us
  other arithmetic: 149 us -> 186 us
    ppermute x0 -> x4, waiting for transfers between devices: none -> 628 us  [doubled_up(): theirs = lax.ppermute(grown, axis, [(d, d ^ reach) for d in range(ways)])]
    all_gather x1 -> x0, waiting for transfers between devices: 105 us -> none  [per_device(): band_all = lax.all_gather(band_local, 'src', axis=0, tiled=True)]
    select_n x0 -> x4, other arithmetic: none -> 39.3 us  [doubled_up(): grown = jnp.where(here & reach == 0, mine_first, theirs_first)]
  transfers between devices with their start and end apart: 1 -> 4, of which waited for: 1 -> 4; matrix products, arithmetic and copies ran while one was open for 0% -> 0% of each run, Pallas kernels for 0% -> 0%
where the time goes in v1:
time: 1630 us; the launch traced here: 1620 us
  waiting for transfers between devices  628 us (39%)
  blocking collectives  392 us (24%)
  local copies, waits for them, and re-layouts  369 us (23%)
  other arithmetic  186 us (11%)
  matrix products  34.8 us (2%)
    ppermute x4, waiting for transfers between devices, doubled_up(): theirs = lax.ppermute(grown, axis, [(d, d ^ reach) for d in range(ways)])  628 us
    all_to_all x1, blocking collectives, per_device(): lax.all_to_all(rows_result, 'src', split_axis=2, concat_axis=1, tiled=True)  369 us
    while x792, local copies, waits for them, and re-layouts  145 us
    dynamic_update_slice x64, other arithmetic, one_group(): lax.dynamic_update_slice(output, column, (jnp.int32(0), jnp.int32(0), j *...  48 us
    neg x64, other arithmetic, block_column(): -right_im  46.7 us
    while x2, local copies, waits for them, and re-layouts, per_device(): lax.fori_loop(0, block_count // 8, one_group, jnp.zeros((2, row_count, bl...  41 us
    all_to_all x1, local copies, waits for them, and re-layouts, per_device(): lax.all_to_all(rows_result, 'src', split_axis=2, concat_axis=1, tiled=True)  40.8 us
    mul x64, other arithmetic, block_column(): left_all = left_all * mask_col.astype(jnp.bfloat16)[None, :, None, :, None]  39.8 us
  transfers between devices with their start and end apart: 4, of which 4 were waited for; matrix products, arithmetic and copies ran while one was open for 0% of the time, Pallas kernels for 0%

profile of v1, /device:TPU:1, one launch (start us, length us, event | category | flops | bytes accessed | tf_op | source)
XLA Modules:
  0.0 1617.4 jit_solution(2591521802966731921)
XLA Ops:
  0.8 23.3 %all-gather = f32[16,1,512]{2,1,0:T(1,128)S(1)} all-gather(f32[1,1,512]{2,1,0:T(1,128)} %bitcast.656), channel_id=1, replica_groups=mesh['freq'=2,'src'=16] {'src'}, dimensions={0}, use_global_device_ids=true | all-gather | bytes 34816 | tf_op jit(solution)/shard_map/all_gather | solution.py:56
  24.0 11.8 fusion.144
  35.8 11.9 copy.114
  47.7 11.9 copy.113
  59.7 8.8 fusion.129
  68.4 3.3 multiply_convert_fusion
  71.8 5.8 copy-done
  81.5 2.8 collective-permute-done
  84.3 2.0 constant_dynamic-update-slice_fusion.129
  86.9 58.4 %collective-permute-done.1 = bf16[8,5,2,128,128]{4,3,2,1,0:T(8,128)(2,1)} collective-permute-done((bf16[8,5,2,128,128]{4,3,2,1,0:T(8,128)(2,1)S(1)}, bf16[8,5,2,128,128]{4,3,2,1,0:T(8,128)(2,1)}, u32[]{:S(2)}, u32[]{:S(2)}) %collective-permute-start.1) | collective-permute-done | bytes 2621472 | tf_op jit(solution)/shard_map/ppermute | solution.py:14
  145.3 5.7 maximum_select_fusion.2
  151.0 113.9 %collective-permute-done.2 = bf16[16,5,2,128,128]{4,3,2,1,0:T(8,128)(2,1)} collective-permute-done((bf16[16,5,2,128,128]{4,3,2,1,0:T(8,128)(2,1)}, bf16[16,5,2,128,128]{4,3,2,1,0:T(8,128)(2,1)}, u32[]{:S(2)}, u32[]{:S(2)}) %collective-permute-start.2) | collective-permute-done | bytes 5242912 | tf_op jit(solution)/shard_map/ppermute | solution.py:14
  264.9 12.4 maximum_select_fusion.1
  277.6 452.9 %collective-permute-done.3 = bf16[32,5,2,128,128]{4,3,2,1,0:T(8,128)(2,1)} collective-permute-done((bf16[32,5,2,128,128]{4,3,2,1,0:T(8,128)(2,1)}, bf16[32,5,2,128,128]{4,3,2,1,0:T(8,128)(2,1)}, u32[]{:S(2)}, u32[]{:S(2)}) %collective-permute-start.3) | collective-permute-done | bytes 10485792 | tf_op jit(solution)/shard_map/ppermute | solution.py:14
  730.5 20.9 %maximum_select_fusion = bf16[64,5,2,128,128]{4,3,2,1,0:T(8,128)(2,1)} fusion(bf16[32,5,2,128,128]{4,3,2,1,0:T(8,128)(2,1)} %collective-permute-done.3, bf16[32,5,2,128,128]{4,3,2,1,0:T(8,128)(2,1)} %maximum_select_fusion.1, pred[]{:T(512)S(6)} %eq.28), kind=kLoop, calls=%fused_computation.401 | loop fusion | flops 31457280 | bytes 41943040 | tf_op jit(solution)/shard_map/jit(_where)/select_n | solution.py:17
  751.4 6.1 broadcast_in_dim.36
  757.4 409.7 %while.18 = (s32[]{:T(128)}, bf16[2,512,8192]{2,1,0:T(8,128)(2,1)}, bf16[2,512,8192]{1,2,0:T(8,128)(2,1)}, pred[4,64,5]{2,0,1:T(4,128)(4,1)S(1)}, bf16[64,5,2,12...) while((s32[]{:T(128)}, bf16[2,512,8192]{2,1,0:T(8,128)(2,1)}, ...), condition=%wide.region_2.3_spmd, body=%wide.region_1.2_spmd.sunk | while | flops 2735341824 | bytes 156504944 | solution.py:104
  761.8 1.2 constant_dynamic-update-slice_fusion.160
  773.3 2.1 constant_dynamic-slice_fusion.41
  813.0 1.2 constant_dynamic-update-slice_fusion.160
  824.5 2.1 constant_dynamic-slice_fusion.41
  864.2 1.2 constant_dynamic-update-slice_fusion.160
  875.7 2.1 constant_dynamic-slice_fusion.41
  915.4 1.2 constant_dynamic-update-slice_fusion.160
  926.9 2.1 constant_dynamic-slice_fusion.41
  978.1 2.1 constant_dynamic-slice_fusion.41
  1029.3 2.1 constant_dynamic-slice_fusion.41
  1080.5 2.1 constant_dynamic-slice_fusion.41
  1131.7 2.1 constant_dynamic-slice_fusion.41
  1167.1 40.9 %copy.111 = bf16[2,512,8192]{1,0,2:T(2,128)(2,1)} copy(bf16[2,512,8192]{2,1,0:T(8,128)(2,1)} %get-tuple-element.323) | data formatting | bytes 33554432 | tf_op jit(solution)/shard_map/while | solution.py:104
  1208.0 368.6 %all_to_all.18 = bf16[2,512,8192]{1,0,2:T(2,128)(2,1)} all-to-all(bf16[2,512,8192]{1,0,2:T(2,128)(2,1)} %copy.111), channel_id=1, replica_groups=mesh['freq'=2,'src'=16] {'src'}, dimensions={2} | all-to-all | bytes 33554432 | tf_op jit(solution)/shard_map/all_to_all | solution.py:107
  1576.6 40.8 %copy.112 = bf16[2,16,512,512]{3,2,1,0:T(8,128)(2,1)} copy(bf16[2,16,512,512]{2,0,3,1:T(2,128)(2,1)} %bitcast.632) | data formatting | bytes 33554432 | tf_op jit(solution)/shard_map/all_to_all | solution.py:107
  (1483 shorter events, 386.6 us)
Async XLA Ops:
  71.8 5.8 copy-start
  81.1 3.2 collective-permute-start
  86.8 58.5 %collective-permute-start.1 = (bf16[8,5,2,128,128]{4,3,2,1,0:T(8,128)(2,1)S(1)}, bf16[8,5,2,128,128]{4,3,2,1,0:T(8,128)(2,1)}, u32[]{:S(2)}, u32[]{:S(2)}) collective-permute-start(bf16[8,5,2,128,128]{4,3,2,1,0:T(8,128)(2,1)S(1)} %broadcast_select_fusion), channel_id=1, source_target_pairs={{0,2},{1,3},{2,0},{3,1},{4,6},{5,7},{6,4},{7,5},{8,10},{9,11},{10,... | collective-permute-start | bytes 7864328 | tf_op jit(solution)/shard_map/ppermute | solution.py:14
  151.0 113.9 %collective-permute-start.2 = (bf16[16,5,2,128,128]{4,3,2,1,0:T(8,128)(2,1)}, bf16[16,5,2,128,128]{4,3,2,1,0:T(8,128)(2,1)}, u32[]{:S(2)}, u32[]{:S(2)}) collective-permute-start(bf16[16,5,2,128,128]{4,3,2,1,0:T(8,128)(2,1)} %maximum_select_fusion.2), channel_id=1, source_target_pairs={{0,4},{1,5},{2,6},{3,7},{4,0},{5,1},{6,2},{7,3},{8,12},{9,13},{10,... | collective-permute-start | bytes 15728648 | tf_op jit(solution)/shard_map/ppermute | solution.py:14
  151.0 126.4 %copy-start.41 = (s32[4,64,4]{1,2,0:T(4,128)S(1)}, s32[4,64,4]{1,2,0:T(4,128)}, u32[]{:S(2)}) copy-start(s32[4,64,4]{1,2,0:T(4,128)} %param.9) | copy-start | bytes 12292
  277.3 453.2 %collective-permute-start.3 = (bf16[32,5,2,128,128]{4,3,2,1,0:T(8,128)(2,1)}, bf16[32,5,2,128,128]{4,3,2,1,0:T(8,128)(2,1)}, u32[]{:S(2)}, u32[]{:S(2)}) collective-permute-start(bf16[32,5,2,128,128]{4,3,2,1,0:T(8,128)(2,1)} %maximum_select_fusion.1), channel_id=1, source_target_pairs={{0,8},{1,9},{2,10},{3,11},{4,12},{5,13},{6,14},{7,15},{8,0},{9,1},... | collective-permute-start | bytes 31457288 | tf_op jit(solution)/shard_map/ppermute | solution.py:14
  763.0 4.7 copy-start.13
  763.0 4.7 copy-start.15
  763.0 4.7 copy-start.37
  763.0 4.7 copy-start.39
  766.6 5.2 copy-start.35
  814.2 4.7 copy-start.13
  814.2 4.7 copy-start.15
  814.2 4.7 copy-start.37
  814.2 4.7 copy-start.39
  817.8 5.3 copy-start.35
  865.4 4.7 copy-start.13
  865.4 4.7 copy-start.15
  865.4 4.7 copy-start.37
  865.4 4.7 copy-start.39
  869.0 5.2 copy-start.35
  916.6 4.7 copy-start.13
  916.6 4.7 copy-start.15
  916.6 4.7 copy-start.37
  916.6 4.7 copy-start.39
  920.2 5.2 copy-start.35
  967.8 4.7 copy-start.13
  967.8 4.7 copy-start.15
  971.4 5.2 copy-start.35
  1022.6 5.2 copy-start.35
  1073.8 5.2 copy-start.35
  1124.9 5.3 copy-start.35
  (294 other events, 583.7 us)

commit v2 on v0

--- a/solution.py
+++ b/solution.py
@@ -92,7 +92,12 @@
     rows_result = lax.fori_loop(
         0, block_count // 8, one_group, jnp.zeros((2, row_count, block_count * BLK), jnp.bfloat16)
     )
-    return lax.all_to_all(rows_result, "src", split_axis=2, concat_axis=1, tiled=True)
+    return jnp.concatenate(
+        lax.all_to_all(
+            jnp.stack(jnp.split(rows_result, lax.axis_size("src"), axis=2)), "src", 0, 0
+        ),
+        axis=1,
+    )
 
 
 def solution(mesh):

time: 1080 us -> 1020 us (0.944)
  local copies, waits for them, and re-layouts: 367 us -> 313 us
    while x2 -> x1, local copies, waits for them, and re-layouts: 41 us -> 0.15 us  [per_device(): lax.fori_loop(0, block_count // 8, one_group, jnp.zeros((2, row_count, bl...]
    all_to_all x1 -> x0, local copies, waits for them, and re-layouts: 40.8 us -> none  [per_device(): lax.all_to_all(rows_result, 'src', split_axis=2, concat_axis=1, tiled=True)]
    unnamed x22 -> x37, local copies, waits for them, and re-layouts: 30.5 us -> 49.9 us
where the time goes in v2:
time: 1020 us; the launch traced here: 1010 us
  blocking collectives  390 us (38%)
  local copies, waits for them, and re-layouts  313 us (31%)
  other arithmetic  149 us (15%)
  waiting for transfers between devices  105 us (10%)
  matrix products  35 us (3%)
  between operations  13.7 us (1%)
    all_to_all x1, blocking collectives, per_device(): lax.all_to_all(jnp.stack(jnp.split(rows_result, lax.axis_size('src'), axi...  367 us
    while x792, local copies, waits for them, and re-layouts  145 us
    all_gather x1, waiting for transfers between devices, per_device(): band_all = lax.all_gather(band_local, 'src', axis=0, tiled=True)  105 us
    unnamed x37, local copies, waits for them, and re-layouts  49.9 us
    dynamic_update_slice x64, other arithmetic, one_group(): lax.dynamic_update_slice(output, column, (jnp.int32(0), jnp.int32(0), j *...  48 us
    neg x64, other arithmetic, block_column(): -right_im  47.3 us
    mul x64, other arithmetic, block_column(): left_all = left_all * mask_col.astype(jnp.bfloat16)[None, :, None, :, None]  39.8 us
    dot_general x64, matrix products, block_column(): product = jnp.dot(left_big, right_big, preferred_element_type=jnp.float32)  35 us
  transfers between devices with their start and end apart: 1, of which 1 were waited for; matrix products, arithmetic and copies ran while one was open for 0% of the time, Pallas kernels for 0%

profile of v2, /device:TPU:1, one launch (start us, length us, event | category | flops | bytes accessed | tf_op | source)
XLA Modules:
  0.0 1012.6 jit_solution(14326913611004952995)
XLA Ops:
  7.3 23.3 %all-gather = f32[16,1,512]{2,1,0:T(1,128)S(1)} all-gather(f32[1,1,512]{2,1,0:T(1,128)} %bitcast.678), channel_id=1, replica_groups=mesh['freq'=2,'src'=16] {'src'}, dimensions={0}, use_global_device_ids=true | all-gather | bytes 34816 | tf_op jit(solution)/shard_map/all_gather | solution.py:44
  30.6 11.8 %fusion.144 = (bf16[1,512,8192]{2,1,0:T(8,128)(2,1)}, bf16[1,512,8192]{2,1,0:T(8,128)(2,1)}) fusion(bf16[2,512,8192]{2,1,0:T(8,128)(2,1)} %param.6), kind=kLoop, calls=%fused_computation.477 | loop fusion | bytes 33554432 | tf_op jit(solution)/shard_map/slice | solution.py:36
  42.4 11.9 %copy.112 = bf16[1,512,8192]{1,2,0:T(8,128)(2,1)} copy(bf16[1,512,8192]{2,1,0:T(8,128)(2,1)} %get-tuple-element.547) | data formatting | bytes 16777216
  54.3 11.9 %copy.111 = bf16[1,512,8192]{1,2,0:T(8,128)(2,1)} copy(bf16[1,512,8192]{2,1,0:T(8,128)(2,1)} %get-tuple-element.548) | data formatting | bytes 16777216
  66.2 8.8 fusion.129
  75.0 3.3 multiply_convert_fusion
  78.3 5.8 copy-done
  89.6 105.3 %all-gather.3.cloned.1.call-done = bf16[64,5,2,128,128]{4,3,2,1,0:T(8,128)(2,1)} async-done(((bf16[4,5,2,128,128]{4,3,2,1,0:T(8,128)(2,1)}), bf16[64,5,2,128,128]{4,3,2,1,0:T(8,128)(2,1)}) %all-gather.3.cloned.1.call-update) | async-done | bytes 20971536 | tf_op jit(solution)/shard_map/all_gather | solution.py:62
  194.9 6.1 broadcast_in_dim.36
  201.0 410.5 %while.18 = (s32[]{:T(128)}, bf16[2,512,8192]{2,1,0:T(8,128)(2,1)}, bf16[2,512,8192]{1,2,0:T(8,128)(2,1)}, pred[4,64,5]{2,0,1:T(4,128)(4,1)S(1)}, bf16[64,5,2,12...) while((s32[]{:T(128)}, bf16[2,512,8192]{2,1,0:T(8,128)(2,1)}, ...), condition=%wide.region_2.3_spmd, body=%wide.region_1.2_spmd.sunk | while | flops 2735341824 | bytes 156504944 | solution.py:92
  216.9 2.1 constant_dynamic-slice_fusion.41
  268.2 2.1 constant_dynamic-slice_fusion.41
  319.5 2.1 constant_dynamic-slice_fusion.41
  370.8 2.1 constant_dynamic-slice_fusion.41
  422.1 2.1 constant_dynamic-slice_fusion.41
  473.5 2.1 constant_dynamic-slice_fusion.41
  524.8 2.1 constant_dynamic-slice_fusion.41
  576.1 2.1 constant_dynamic-slice_fusion.41
  612.8 1.3 bitcast_dynamic-update-slice_fusion.14
  614.1 1.3 bitcast_dynamic-update-slice_fusion.13
  615.4 1.3 bitcast_dynamic-update-slice_fusion.12
  616.7 1.3 bitcast_dynamic-update-slice_fusion.11
  618.0 1.3 bitcast_dynamic-update-slice_fusion.10
  619.3 1.3 bitcast_dynamic-update-slice_fusion.9
  620.6 1.3 bitcast_dynamic-update-slice_fusion.8
  621.9 1.3 bitcast_dynamic-update-slice_fusion.7
  624.5 1.3 bitcast_dynamic-update-slice_fusion.5
  625.8 1.3 bitcast_dynamic-update-slice_fusion.4
  628.4 1.3 bitcast_dynamic-update-slice_fusion.2
  629.7 1.3 bitcast_dynamic-update-slice_fusion.1
  632.3 366.9 %all_to_all.5 = bf16[16,2,512,512]{3,2,1,0:T(8,128)(2,1)S(1)} all-to-all(bf16[16,2,512,512]{3,2,1,0:T(8,128)(2,1)S(1)} %bitcast_dynamic-update-slice_fusion), channel_id=1, replica_groups=mesh['freq'=2,'src'=16] {'src'}, dimensions={0} | all-to-all | bytes 33554432 | tf_op jit(solution)/shard_map/all_to_all | solution.py:96
  999.2 6.5 copy.110
  (1480 shorter events, 398.1 us)
Async XLA Ops:
  6.5 188.4 %all-gather.3.cloned.1.call-start = ((), (), s32[]{:S(2)}) async-start(), calls=%async_computation.1 | async-start | bytes 22282240 | tf_op jit(solution)/shard_map/all_gather | solution.py:62
  78.3 5.8 copy-start
  206.5 4.7 copy-start.13
  206.5 4.7 copy-start.15
  206.5 4.7 copy-start.37
  206.6 4.7 copy-start.39
  210.2 5.3 copy-start.35
  257.8 4.7 copy-start.13
  257.8 4.7 copy-start.15
  257.9 4.7 copy-start.37
  257.9 4.7 copy-start.39
  261.5 5.3 copy-start.35
  312.8 5.3 copy-start.35
  364.1 5.3 copy-start.35
  411.7 4.7 copy-start.13
  411.8 4.7 copy-start.15
  411.8 4.7 copy-start.37
  411.8 4.7 copy-start.39
  415.4 5.3 copy-start.35
  463.1 4.7 copy-start.13
  463.1 4.7 copy-start.15
  463.1 4.7 copy-start.37
  463.1 4.7 copy-start.39
  466.7 5.3 copy-start.35
  514.4 4.8 copy-start.13
  514.4 4.8 copy-start.15
  514.4 4.8 copy-start.37
  514.4 4.8 copy-start.39
  518.0 5.3 copy-start.35
  565.7 4.7 copy-start.13
  565.7 4.7 copy-start.15
  569.3 5.3 copy-start.35
  (291 other events, 569.2 us)
Sparse Core Ops, SparseCore 0:
  88.9 106.0 all-gather.2
